TPU v7x, 32 devices: a whole 2x2x4 slice. The times are simulated.
32 devices in a mesh: fsdp: 4 (over z), ctx: 2 (over x), tp: 4 (over y, core).
Axes of the slice: x: 2, y: 2, z: 4, core: 2. Of those that a mesh axis runs over, the one named last changes fastest.
Arguments:
- resid_in: float32 [4, 2048, 1024], P('fsdp', 'ctx'), may hold values from -6 to 6
- segment_ids: int32 [4, 2048], P('fsdp'), may hold values from 0 to 5, never falling along the last dimension, each value on 1 to 768 neighbouring positions
- cotangent: float32 [4, 2048, 1024], P('fsdp', 'ctx'), may hold values from -6 to 6
- w_factor_a: float32 [1, 1024, 160], P(None, ('fsdp', 'ctx'), 'tp'), may hold values from -0.5 to 0.5
- w_factor_b: float32 [1, 1024, 640], P(None, ('fsdp', 'ctx', 'tp')), may hold values from -0.1875 to 0.1875
- w_out: float32 [1, 1024, 1024], P(None, 'tp', ('fsdp', 'ctx')), may hold values from -0.375 to 0.375
- w_gate_up: float32 [1, 2, 1024, 2816], P(None, None, ('fsdp', 'ctx'), 'tp'), may hold values from -0.1875 to 0.1875
- w_down: float32 [1, 2816, 1024], P(None, 'tp', ('fsdp', 'ctx')), may hold values from -0.109375 to 0.109375
- attn_gains: float32 [1, 1024], P(None, ('fsdp', 'ctx', 'tp')), may hold values from 0.25 to 1.75
- ffn_gains: float32 [1, 1024], P(None, ('fsdp', 'ctx', 'tp')), may hold values from 0.25 to 1.75
Outputs:
- block_out: float32 [4, 2048, 1024], P('fsdp', 'ctx')
- resid_grad: float32 [4, 2048, 1024], P('fsdp', 'ctx')
- grad_factor_a: float32 [1, 1024, 160], P(None, ('fsdp', 'ctx'), 'tp')
- grad_factor_b: float32 [1, 1024, 640], P(None, ('fsdp', 'ctx', 'tp'))
- grad_out: float32 [1, 1024, 1024], P(None, 'tp', ('fsdp', 'ctx'))
- grad_gate_up: float32 [1, 2, 1024, 2816], P(None, None, ('fsdp', 'ctx'), 'tp')
- grad_down: float32 [1, 2816, 1024], P(None, 'tp', ('fsdp', 'ctx'))
- grad_attn_gains: float32 [1, 1024], P(None, ('fsdp', 'ctx', 'tp'))
- grad_ffn_gains: float32 [1, 1024], P(None, ('fsdp', 'ctx', 'tp'))
Inputs may be any that keep to these rules, and one draw needn't show every extreme that they name: `segment_ids`: along each row the ids never fall and run through all 6 documents; each document holds 1 to 768 tokens.
All inputs are finite; a program needn't handle non-finite values.
Results may differ from a plain program's by a relative error of at most 0.024.
The roundings to bfloat16 on the way count: a program that leaves them out, or rounds other values in their place, can miss the bound.
Values may be sent and summed in bfloat16 or wider, within the bound.
No kernel may reach another device: no remote copies, remote signals or barrier semaphores. Data moves between devices by JAX's collectives and lax.ppermute only.
A program may use at most 192 MiB of HBM per device.

v0:
```python
import math

import jax
import jax.numpy as jnp
from jax import lax
from jax.sharding import PartitionSpec as P

HEAD_DIM = 64
RANK_Q = 6
RANK_KV = 2
QUERY_BLOCK = 512
RANKS = 10


EPSILON = 1e-05
PRECISE = lax.Precision.HIGHEST


def doc_positions(segment_ids):
    length = segment_ids.shape[-1]
    token_index = jnp.broadcast_to(jnp.arange(length, dtype=jnp.int32), segment_ids.shape)
    changed = jnp.concatenate(
        [
            jnp.ones(segment_ids.shape[:-1] + (1,), dtype=bool),
            segment_ids[..., 1:] != segment_ids[..., :-1],
        ],
        axis=-1,
    )
    doc_start = lax.cummax(jnp.where(changed, token_index, 0), axis=segment_ids.ndim - 1)
    return (token_index - doc_start).astype(jnp.float32)


def rotate(field_value, positions, direction):
    half_width = field_value.shape[-1] // 2
    frequency = 10000.0 ** (
        -2.0 * jnp.arange(half_width, dtype=jnp.float32) / field_value.shape[-1]
    )
    angles = positions[..., None, None] * frequency
    cosine = jnp.cos(angles)
    sine_part = direction * jnp.sin(angles)
    lower_half = field_value[..., :half_width]
    upper_half = field_value[..., half_width:]
    return jnp.concatenate(
        [
            lower_half * cosine - upper_half * sine_part,
            lower_half * sine_part + upper_half * cosine,
        ],
        axis=-1,
    )


def inverse_rms(values):
    return lax.rsqrt(jnp.mean(values * values, axis=-1, keepdims=True) + EPSILON)


def norm_back(grad_value, values, inverse, gain):
    scaled = grad_value * gain.astype(jnp.float32)
    normal = values * inverse
    return inverse * (scaled - normal * jnp.mean(scaled * normal, axis=-1, keepdims=True))


def fetch_split(layer_index, w_factor_a, w_out, w_gate_up, w_down):
    return (
        lax.all_gather(
            w_factor_a[layer_index].astype(jnp.bfloat16), ("fsdp", "ctx"), axis=0, tiled=True
        ),
        lax.all_gather(
            w_out[layer_index].astype(jnp.bfloat16), ("fsdp", "ctx"), axis=1, tiled=True
        ),
        lax.all_gather(
            w_gate_up[layer_index].astype(jnp.bfloat16), ("fsdp", "ctx"), axis=1, tiled=True
        ),
        lax.all_gather(
            w_down[layer_index].astype(jnp.bfloat16), ("fsdp", "ctx"), axis=1, tiled=True
        ),
    )


def fetch_shared(layer_index, w_factor_b, attn_gains, ffn_gains):
    return (
        lax.all_gather(
            w_factor_b[layer_index].astype(jnp.bfloat16), ("fsdp", "ctx", "tp"), axis=0, tiled=True
        ),
        lax.all_gather(
            attn_gains[layer_index].astype(jnp.bfloat16), ("fsdp", "ctx", "tp"), axis=0, tiled=True
        ),
        lax.all_gather(
            ffn_gains[layer_index].astype(jnp.bfloat16), ("fsdp", "ctx", "tp"), axis=0, tiled=True
        ),
    )


def fetch_split_again(layer_index, w_factor_a, w_out, w_gate_up, w_down):
    return (
        lax.all_gather(
            w_factor_a[layer_index].astype(jnp.bfloat16), ("fsdp", "ctx"), axis=0, tiled=True
        ),
        lax.all_gather(
            w_out[layer_index].astype(jnp.bfloat16), ("fsdp", "ctx"), axis=1, tiled=True
        ),
        lax.all_gather(
            w_gate_up[layer_index].astype(jnp.bfloat16), ("fsdp", "ctx"), axis=1, tiled=True
        ),
        lax.all_gather(
            w_down[layer_index].astype(jnp.bfloat16), ("fsdp", "ctx"), axis=1, tiled=True
        ),
    )


def fetch_shared_again(layer_index, w_factor_b, attn_gains, ffn_gains):
    return (
        lax.all_gather(
            w_factor_b[layer_index].astype(jnp.bfloat16), ("fsdp", "ctx", "tp"), axis=0, tiled=True
        ),
        lax.all_gather(
            attn_gains[layer_index].astype(jnp.bfloat16), ("fsdp", "ctx", "tp"), axis=0, tiled=True
        ),
        lax.all_gather(
            ffn_gains[layer_index].astype(jnp.bfloat16), ("fsdp", "ctx", "tp"), axis=0, tiled=True
        ),
    )


def branch_total(partial_value):
    return lax.psum(partial_value.astype(jnp.bfloat16), "tp").astype(jnp.float32)


def grad_total(partial_value):
    return lax.psum(partial_value.astype(jnp.bfloat16), "tp").astype(jnp.float32)


def gain_term(partial_value, values, inverse):
    return jnp.sum(partial_value * values * inverse, axis=0)


def build_query(a_raw, b_raw, positions_here):
    b_query = rotate(b_raw[:, :, :RANK_Q], positions_here, 1.0)
    query = (
        jnp.einsum("slhr,slrd->slhd", a_raw[..., :RANK_Q], b_query, precision=PRECISE) / RANK_Q
    ).astype(jnp.bfloat16)
    return (query, b_query)


def build_keys(a_all, b_all, heads_here):
    seq_count, full_len = (a_all.shape[0], a_all.shape[1])
    a_four = a_all.reshape(seq_count, full_len, heads_here, 2 * RANK_KV).astype(jnp.float32)
    b_four = b_all.reshape(seq_count, full_len, 2 * RANK_KV, HEAD_DIM).astype(jnp.float32)
    key_rows = (
        jnp.einsum(
            "slhr,slrd->slhd", a_four[..., :RANK_KV], b_four[:, :, :RANK_KV], precision=PRECISE
        )
        / RANK_KV
    )
    value_rows = (
        jnp.einsum(
            "slhr,slrd->slhd", a_four[..., RANK_KV:], b_four[:, :, RANK_KV:], precision=PRECISE
        )
        / RANK_KV
    )
    return (key_rows.astype(jnp.bfloat16), value_rows.astype(jnp.bfloat16), a_four, b_four)


def block_scores(query_block, key_rows, allowed_block):
    scores = jnp.einsum(
        "qhd,khd->hqk", query_block, key_rows, preferred_element_type=jnp.float32
    ) / math.sqrt(HEAD_DIM)
    return jnp.where(allowed_block[None], scores, -1e30)


def attend_forward(query_block, key_rows, value_rows, allowed_block):
    scores = block_scores(query_block, key_rows, allowed_block)
    row_max = jnp.max(scores, axis=-1, keepdims=True)
    exp_scores = jnp.exp(scores - row_max)
    row_total = jnp.sum(exp_scores, axis=-1, keepdims=True)
    attn_probs = (exp_scores / row_total).astype(jnp.bfloat16)
    attn_mixed = jnp.einsum(
        "hqk,khd->qhd", attn_probs, value_rows, preferred_element_type=jnp.float32
    ).astype(jnp.bfloat16)
    return (attn_mixed, row_max + jnp.log(row_total))


def attend_sequence(packed):
    query, key_rows, value_rows, allowed_rows = packed
    local_len, heads_here, head_width = query.shape
    block_count = local_len // QUERY_BLOCK

    def one_block(block_data):
        return attend_forward(block_data[0], key_rows, value_rows, block_data[1])

    attn_mixed, log_total = lax.map(
        one_block,
        (
            query.reshape(block_count, QUERY_BLOCK, heads_here, head_width),
            allowed_rows.reshape(block_count, QUERY_BLOCK, allowed_rows.shape[1]),
        ),
    )
    return (attn_mixed.reshape(local_len, heads_here, head_width), log_total)


def attend_sequence_back(packed):
    query, key_rows, value_rows, allowed_rows, log_total, grad_mixed = packed
    local_len, heads_here, head_width = query.shape
    block_count = local_len // QUERY_BLOCK

    def one_block(running, block_data):
        query_block, allowed_block, log_block, grad_block = block_data
        scores = block_scores(query_block, key_rows, allowed_block)
        attn_probs = jnp.exp(scores - log_block)
        grad_probs = jnp.einsum(
            "qhd,khd->hqk", grad_block, value_rows, preferred_element_type=jnp.float32
        )
        row_inner = jnp.sum(attn_probs * grad_probs, axis=-1, keepdims=True)
        grad_scores = (attn_probs * (grad_probs - row_inner)).astype(jnp.bfloat16)
        grad_values = jnp.einsum(
            "hqk,qhd->khd",
            attn_probs.astype(jnp.bfloat16),
            grad_block,
            preferred_element_type=jnp.float32,
        )
        grad_query = jnp.einsum(
            "hqk,khd->qhd", grad_scores, key_rows, preferred_element_type=jnp.float32
        ) / math.sqrt(HEAD_DIM)
        grad_keys = jnp.einsum(
            "hqk,qhd->khd", grad_scores, query_block, preferred_element_type=jnp.float32
        ) / math.sqrt(HEAD_DIM)
        return ((running[0] + grad_keys, running[1] + grad_values), grad_query)

    zero_keys = jnp.zeros(key_rows.shape, jnp.float32)
    blocks = (
        query.reshape(block_count, QUERY_BLOCK, heads_here, head_width),
        allowed_rows.reshape(block_count, QUERY_BLOCK, allowed_rows.shape[1]),
        log_total,
        grad_mixed.reshape(block_count, QUERY_BLOCK, heads_here, head_width),
    )
    (grad_keys, grad_values), grad_query = lax.scan(one_block, (zero_keys, zero_keys), blocks)
    return (grad_query.reshape(local_len, heads_here, head_width), grad_keys, grad_values)


def layer_forward(stream, split_w, shared_w, positions_here, allowed, seq_count):
    weight_a, weight_o, weight_gu, weight_d = split_w
    weight_b, gain_attn, gain_ffn = shared_w
    inverse_attn = inverse_rms(stream)
    normed = (stream * inverse_attn * gain_attn.astype(jnp.float32)).astype(jnp.bfloat16)
    row_count = normed.shape[0]
    local_len = row_count // seq_count
    heads_here = weight_a.shape[1] // RANKS
    a_raw = jnp.dot(normed, weight_a, preferred_element_type=jnp.float32).reshape(
        seq_count, local_len, heads_here, RANKS
    )
    b_raw = jnp.dot(normed, weight_b, preferred_element_type=jnp.float32).reshape(
        seq_count, local_len, RANKS, HEAD_DIM
    )
    query, b_query = build_query(a_raw, b_raw, positions_here)
    a_send = (
        a_raw[..., RANK_Q:]
        .astype(jnp.bfloat16)
        .reshape(seq_count, local_len, heads_here * 2 * RANK_KV)
    )
    b_send = (
        jnp.concatenate(
            [
                rotate(b_raw[:, :, RANK_Q : RANK_Q + RANK_KV], positions_here, 1.0),
                b_raw[:, :, RANK_Q + RANK_KV :],
            ],
            axis=2,
        )
        .astype(jnp.bfloat16)
        .reshape(seq_count, local_len, 2 * RANK_KV * HEAD_DIM)
    )
    a_all, b_all = (
        lax.all_gather(a_send, "ctx", axis=1, tiled=True),
        lax.all_gather(b_send, "ctx", axis=1, tiled=True),
    )
    key_rows, value_rows, a_four, b_four = build_keys(a_all, b_all, heads_here)
    attn_mixed, log_total = lax.map(attend_sequence, (query, key_rows, value_rows, allowed))
    mixed_flat = attn_mixed.reshape(row_count, heads_here * HEAD_DIM)
    mid_stream = stream + branch_total(
        jnp.dot(mixed_flat, weight_o, preferred_element_type=jnp.float32)
    )
    inverse_ffn = inverse_rms(mid_stream)
    normed_ffn = (mid_stream * inverse_ffn * gain_ffn.astype(jnp.float32)).astype(jnp.bfloat16)
    gate_proj = jnp.dot(normed_ffn, weight_gu[0], preferred_element_type=jnp.float32)
    up_proj = jnp.dot(normed_ffn, weight_gu[1], preferred_element_type=jnp.float32)
    activated = (jax.nn.silu(gate_proj) * up_proj).astype(jnp.bfloat16)
    layer_out = mid_stream + branch_total(
        jnp.dot(activated, weight_d, preferred_element_type=jnp.float32)
    )
    saved = (
        stream,
        inverse_attn,
        normed,
        a_raw,
        b_raw,
        a_all,
        b_all,
        mixed_flat,
        log_total,
        mid_stream,
        inverse_ffn,
        normed_ffn,
        gate_proj,
        up_proj,
        activated,
    )
    return (layer_out, saved)


def layer_backward(grad_stream, split_w, shared_w, saved, positions_here, allowed, seq_count):
    weight_a, weight_o, weight_gu, weight_d = split_w
    weight_b, gain_attn, gain_ffn = shared_w
    (
        stream,
        inverse_attn,
        normed,
        a_raw,
        b_raw,
        a_all,
        b_all,
        mixed_flat,
        log_total,
        mid_stream,
        inverse_ffn,
        normed_ffn,
        gate_proj,
        up_proj,
        activated,
    ) = saved
    row_count = normed.shape[0]
    local_len = row_count // seq_count
    full_len = a_all.shape[1]
    heads_here = weight_a.shape[1] // RANKS
    grad_branch = grad_stream.astype(jnp.bfloat16)
    grad_down = jnp.einsum("rf,rd->fd", activated, grad_branch, preferred_element_type=jnp.float32)
    grad_act = jnp.einsum("rd,fd->rf", grad_branch, weight_d, preferred_element_type=jnp.float32)
    gate_sigmoid = jax.nn.sigmoid(gate_proj)
    grad_gate = (
        grad_act * up_proj * gate_sigmoid * (1.0 + gate_proj * (1.0 - gate_sigmoid))
    ).astype(jnp.bfloat16)
    grad_up = (grad_act * gate_proj * gate_sigmoid).astype(jnp.bfloat16)
    grad_gate_up = jnp.stack(
        [
            jnp.einsum("rd,rf->df", normed_ffn, grad_gate, preferred_element_type=jnp.float32),
            jnp.einsum("rd,rf->df", normed_ffn, grad_up, preferred_element_type=jnp.float32),
        ]
    )
    grad_normed_ffn = jnp.einsum(
        "rf,df->rd", grad_gate, weight_gu[0], preferred_element_type=jnp.float32
    ) + jnp.einsum("rf,df->rd", grad_up, weight_gu[1], preferred_element_type=jnp.float32)
    summed_ffn = grad_total(grad_normed_ffn)
    gain_grad_ffn = gain_term(grad_normed_ffn, mid_stream, inverse_ffn)
    grad_mid = grad_stream + norm_back(summed_ffn, mid_stream, inverse_ffn, gain_ffn)
    grad_attn = grad_mid.astype(jnp.bfloat16)
    grad_out_w = jnp.einsum("ra,rd->ad", mixed_flat, grad_attn, preferred_element_type=jnp.float32)
    grad_mixed = (
        jnp.einsum("rd,ad->ra", grad_attn, weight_o, preferred_element_type=jnp.float32)
        .astype(jnp.bfloat16)
        .reshape(seq_count, local_len, heads_here, HEAD_DIM)
    )
    query, b_query = build_query(a_raw, b_raw, positions_here)
    key_rows, value_rows, a_four, b_four = build_keys(a_all, b_all, heads_here)
    grad_query, grad_keys, grad_values = lax.map(
        attend_sequence_back, (query, key_rows, value_rows, allowed, log_total, grad_mixed)
    )
    grad_aq = jnp.einsum("slhd,slrd->slhr", grad_query, b_query, precision=PRECISE) / RANK_Q
    grad_bq = (
        jnp.einsum("slhr,slhd->slrd", a_raw[..., :RANK_Q], grad_query, precision=PRECISE) / RANK_Q
    )
    grad_ak = (
        jnp.einsum("slhd,slrd->slhr", grad_keys, b_four[:, :, :RANK_KV], precision=PRECISE)
        / RANK_KV
    )
    grad_av = (
        jnp.einsum("slhd,slrd->slhr", grad_values, b_four[:, :, RANK_KV:], precision=PRECISE)
        / RANK_KV
    )
    grad_bk = (
        jnp.einsum("slhr,slhd->slrd", a_four[..., :RANK_KV], grad_keys, precision=PRECISE) / RANK_KV
    )
    grad_bv = (
        jnp.einsum("slhr,slhd->slrd", a_four[..., RANK_KV:], grad_values, precision=PRECISE)
        / RANK_KV
    )
    send_a = jnp.concatenate([grad_ak, grad_av], axis=-1).reshape(
        seq_count, full_len, heads_here * 2 * RANK_KV
    )
    send_b = jnp.concatenate([grad_bk, grad_bv], axis=2).reshape(
        seq_count, full_len, 2 * RANK_KV * HEAD_DIM
    )
    back_a, back_b = (
        lax.psum_scatter(
            send_a.astype(jnp.bfloat16), "ctx", scatter_dimension=1, tiled=True
        ).astype(jnp.float32),
        lax.psum_scatter(
            send_b.astype(jnp.bfloat16), "ctx", scatter_dimension=1, tiled=True
        ).astype(jnp.float32),
    )
    back_b = back_b.reshape(seq_count, local_len, 2 * RANK_KV, HEAD_DIM)
    grad_b = (
        jnp.concatenate(
            [
                rotate(grad_bq, positions_here, -1.0),
                rotate(back_b[:, :, :RANK_KV], positions_here, -1.0),
                back_b[:, :, RANK_KV:],
            ],
            axis=2,
        )
        .reshape(row_count, RANKS * HEAD_DIM)
        .astype(jnp.bfloat16)
    )
    grad_a = (
        jnp.concatenate(
            [grad_aq, back_a.reshape(seq_count, local_len, heads_here, 2 * RANK_KV)], axis=-1
        )
        .reshape(row_count, heads_here * RANKS)
        .astype(jnp.bfloat16)
    )
    grad_wa = jnp.einsum("rd,rc->dc", normed, grad_a, preferred_element_type=jnp.float32)
    grad_wb = jnp.einsum("rd,rc->dc", normed, grad_b, preferred_element_type=jnp.float32)
    grad_normed = jnp.einsum(
        "rc,dc->rd", grad_a, weight_a, preferred_element_type=jnp.float32
    ) + jnp.einsum("rc,dc->rd", grad_b, weight_b, preferred_element_type=jnp.float32)
    summed_attn = grad_total(grad_normed)
    gain_grad_attn = gain_term(grad_normed, stream, inverse_attn)
    grad_in = grad_mid + norm_back(summed_attn, stream, inverse_attn, gain_attn)
    return (
        grad_in,
        (grad_wa, grad_out_w, grad_gate_up, grad_down),
        (grad_wb, gain_grad_attn, gain_grad_ffn),
    )


def shards(
    resid_in,
    segment_ids,
    cotangent,
    w_factor_a,
    w_factor_b,
    w_out,
    w_gate_up,
    w_down,
    attn_gains,
    ffn_gains,
):
    seq_count, local_len, model_width = resid_in.shape
    full_len = segment_ids.shape[1]
    layer_count = w_factor_a.shape[0]
    offset = lax.axis_index("ctx") * local_len
    positions_all = doc_positions(segment_ids)
    positions_here = lax.dynamic_slice_in_dim(positions_all, offset, local_len, 1)
    query_segs = lax.dynamic_slice_in_dim(segment_ids, offset, local_len, 1)
    query_index = offset + jnp.arange(local_len, dtype=jnp.int32)
    allowed = (
        jnp.arange(full_len, dtype=jnp.int32)[None, None, :] <= query_index[None, :, None]
    ) & (segment_ids[:, None, :] == query_segs[:, :, None])
    stream = resid_in.reshape(seq_count * local_len, model_width)
    grad_stream = cotangent.reshape(seq_count * local_len, model_width)
    kept = []
    layer_index = 0
    split_w = fetch_split(layer_index, w_factor_a, w_out, w_gate_up, w_down)
    shared_w = fetch_shared(layer_index, w_factor_b, attn_gains, ffn_gains)
    kept.append((split_w, shared_w))
    stream, saved = layer_forward(stream, split_w, shared_w, positions_here, allowed, seq_count)
    saved_all = [saved]
    list_a = [None] * layer_count
    list_b = [None] * layer_count
    list_o = [None] * layer_count
    list_gu = [None] * layer_count
    list_d = [None] * layer_count
    list_attn_gain = [None] * layer_count
    list_ffn_gain = [None] * layer_count
    for layer_index in reversed(range(layer_count)):
        split_w = fetch_split_again(layer_index, w_factor_a, w_out, w_gate_up, w_down)
        shared_w = fetch_shared_again(layer_index, w_factor_b, attn_gains, ffn_gains)
        grad_stream, split_grads, shared_grads = layer_backward(
            grad_stream,
            split_w,
            shared_w,
            saved_all[layer_index],
            positions_here,
            allowed,
            seq_count,
        )
        part_a, part_o, part_gu, part_d = (
            lax.psum_scatter(
                split_grads[0].astype(jnp.bfloat16),
                ("fsdp", "ctx"),
                scatter_dimension=0,
                tiled=True,
            ).astype(jnp.float32),
            lax.psum_scatter(
                split_grads[1].astype(jnp.bfloat16),
                ("fsdp", "ctx"),
                scatter_dimension=1,
                tiled=True,
            ).astype(jnp.float32),
            lax.psum_scatter(
                split_grads[2].astype(jnp.bfloat16),
                ("fsdp", "ctx"),
                scatter_dimension=1,
                tiled=True,
            ).astype(jnp.float32),
            lax.psum_scatter(
                split_grads[3].astype(jnp.bfloat16),
                ("fsdp", "ctx"),
                scatter_dimension=1,
                tiled=True,
            ).astype(jnp.float32),
        )
        part_b, part_attn_gain, part_ffn_gain = (
            lax.psum_scatter(
                shared_grads[0], ("fsdp", "ctx", "tp"), scatter_dimension=0, tiled=True
            ),
            lax.psum_scatter(
                shared_grads[1], ("fsdp", "ctx", "tp"), scatter_dimension=0, tiled=True
            ),
            lax.psum_scatter(
                shared_grads[2], ("fsdp", "ctx", "tp"), scatter_dimension=0, tiled=True
            ),
        )
        list_a[layer_index] = part_a
        list_o[layer_index] = part_o
        list_gu[layer_index] = part_gu
        list_d[layer_index] = part_d
        list_b[layer_index] = part_b
        list_attn_gain[layer_index] = part_attn_gain
        list_ffn_gain[layer_index] = part_ffn_gain
    return (
        stream.reshape(resid_in.shape),
        grad_stream.reshape(resid_in.shape),
        jnp.stack(list_a),
        jnp.stack(list_b),
        jnp.stack(list_o),
        jnp.stack(list_gu),
        jnp.stack(list_d),
        jnp.stack(list_attn_gain),
        jnp.stack(list_ffn_gain),
    )


def solution(mesh):
    return jax.shard_map(
        shards,
        mesh=mesh,
        in_specs=(
            P("fsdp", "ctx", None),
            P("fsdp", None),
            P("fsdp", "ctx", None),
            P(None, ("fsdp", "ctx"), "tp"),
            P(None, ("fsdp", "ctx", "tp"), None),
            P(None, "tp", ("fsdp", "ctx")),
            P(None, None, ("fsdp", "ctx"), "tp"),
            P(None, "tp", ("fsdp", "ctx")),
            P(None, ("fsdp", "ctx", "tp")),
            P(None, ("fsdp", "ctx", "tp")),
        ),
        out_specs=(
            P("fsdp", "ctx", None),
            P("fsdp", "ctx", None),
            P(None, ("fsdp", "ctx"), "tp"),
            P(None, ("fsdp", "ctx", "tp"), None),
            P(None, "tp", ("fsdp", "ctx")),
            P(None, None, ("fsdp", "ctx"), "tp"),
            P(None, "tp", ("fsdp", "ctx")),
            P(None, ("fsdp", "ctx", "tp")),
            P(None, ("fsdp", "ctx", "tp")),
        ),
        check_vma=False,
    )
```

profile of v0, /device:TPU:0, one launch (start us, length us, event | category | flops | bytes accessed | tf_op | source)
XLA Modules:
  0.0 1082.0 jit_solution(16315659433688463502)
XLA Ops:
  11.4 42.0 %all-reduce.5 = (bf16[1024]{0:T(1024)(128)(2,1)S(1)}, bf16[1024]{0:T(1024)(128)(2,1)}) all-reduce(bf16[1024]{0:T(1024)(128)(2,1)S(1)} %dynamic-update-slice, bf16[1024]{0:T(1024)(128)(2,1)S(1)} %dynamic-update-slice.1), channel_id=2, replica_groups=mesh['fsdp'=4,'ctx'=2,'tp'=4] {'fsdp','ctx','tp'}, use_global_device_ids=true, to_apply=%add | all-reduce | flops 2048 | bytes 8192
  57.7 26.0 %all-gather.1 = bf16[1,1024,40]{1,2,0:T(8,128)(2,1)S(1)} all-gather(bf16[1,128,40]{1,2,0:T(8,128)(2,1)S(1)} %convert_element_type.250), channel_id=3, replica_groups=mesh['fsdp'=4,'ctx'=2,'tp'=4] {'fsdp','ctx'}, dimensions={1}, use_global_device_ids=true | all-gather | bytes 92160 | tf_op jit(solution)/shard_map/all_gather | solution.py:64
  110.4 28.9 %all-gather.3 = bf16[1,256,1024]{2,1,0:T(8,128)(2,1)} all-gather(bf16[1,256,128]{2,1,0:T(8,128)(2,1)S(1)} %copy-done.53), channel_id=5, replica_groups=mesh['fsdp'=4,'ctx'=2,'tp'=4] {'fsdp','ctx'}, dimensions={2}, use_global_device_ids=true | all-gather | bytes 589824 | tf_op jit(solution)/shard_map/all_gather | solution.py:67
  146.0 9.6 multiply_convert_fusion.12
  179.9 29.6 %while.47 = (s32[]{:T(128)}, bf16[2,512,4,64]{1,3,2,0:T(8,128)(2,1)}, f32[2,4,512,1]{2,1,3,0:T(4,128)}, pred[2,512,2048]{2,1,0:T(8,128)(4,1)S(1)}, bf16[2,512,4,...) while((s32[]{:T(128)}, ...), condition=%wide.region_6.7_spmd, body=%wide.region_3.6_spmd.sunk | while | flops 1124202496 | bytes 66650304 | solution.py:190
  218.2 49.4 %all-reduce.11.cloned.1.call-done = bf16[1024,1024]{1,0:T(8,128)(2,1)} async-done(((bf16[1024,1024]{1,0:T(8,128)(2,1)}), bf16[1024,1024]{1,0:T(8,128)(2,1)}) %all-reduce.11.cloned.1.call-update) | async-done | bytes 2097168 | tf_op jit(solution)/shard_map/psum | solution.py:125
  287.8 35.3 %all-gather.18.cloned.1.call-done = bf16[1,704,1024]{2,1,0:T(8,128)(2,1)} async-done(((bf16[1,704,128]{2,1,0:T(8,128)(2,1)}), bf16[1,704,1024]{2,1,0:T(8,128)(2,1)}) %all-gather.18.cloned.1.call-update) | async-done | bytes 1441808 | tf_op jit(solution)/shard_map/all_gather | solution.py:73
  337.9 49.7 %all-reduce.13.cloned.1.call-done = bf16[1024,1024]{1,0:T(8,128)(2,1)} async-done(((bf16[1024,1024]{1,0:T(8,128)(2,1)}), bf16[1024,1024]{1,0:T(8,128)(2,1)}) %all-reduce.13.cloned.1.call-update) | async-done | bytes 2097168 | tf_op jit(solution)/shard_map/psum | solution.py:129
  404.7 91.3 %while.48 = (s32[]{:T(128)}, f32[2048,4,64]{0,2,1:T(8,128)}, f32[2048,4,64]{0,2,1:T(8,128)}, f32[2,512,4,64]{1,3,2,0:T(8,128)}, bf16[2,512,4,64]{1,3,2,0:T(8,128...) while((s32[]{:T(128)}, f32[2048,4,64]{0,2,1:T(8,128)}, ...), condition=%wide.region_14.15_spmd.clone, body=%wide.region_12.14_spmd.clone.sunk | while | flops 2750019584 | bytes 202957136 | solution.py:235
  416.5 11.5 %multiply_reduce_fusion.6 = (f32[4,512]{1,0:T(4,128)}, f32[4,512,2048]{2,1,0:T(8,128)}) fusion(f32[4,512,2048]{2,1,0:T(8,128)S(1)} %fusion.174, f32[4,512]{1,0:T(4,128)S(1)} %dynamic-slice_bitcast_fusion.9, pred[512,2048]{1,0:T(8,128)(4,1)} %copy-done.1, bf16[2048,4,64]{0,2,1:T(8,128)(2,1)} %get-tuple-element.484, ...), kind=kOutput, calls=%fused_computation.18.clone.1 | convolution fusion | flops 557840384 | bytes 35930116 | tf_op jit(solution)/shard_map/while/body/eval_jaxpr/while/body/eval_jaxpr/qhd,khd->hqk/dot_general | solution.py:209
  428.0 11.0 %multiply_convert_fusion.14 = bf16[4,512,2048]{2,1,0:T(8,128)(2,1)} fusion(f32[4,512,2048]{2,1,0:T(8,128)} %get-tuple-element.425, f32[4,512,2048]{2,1,0:T(8,128)S(1)} %fusion.174, f32[4,512]{1,0:T(4,128)} %get-tuple-element.426, f32[4,512]{1,0:T(4,128)S(1)} %dynamic-slice_bitcast_fusion.9, pred[512,2048]{1,0:T(8,128)(4,1)} %copy-done.1), kind=kLoop, calls=%fused_computation.17.clone.1 | loop fusion | flops 25165824 | bytes 43008000 | tf_op jit(solution)/shard_map/while/body/eval_jaxpr/while/body/eval_jaxpr/convert_element_type | solution.py:213
  461.7 11.5 %multiply_reduce_fusion.6 = (f32[4,512]{1,0:T(4,128)}, f32[4,512,2048]{2,1,0:T(8,128)}) fusion(f32[4,512,2048]{2,1,0:T(8,128)S(1)} %fusion.174, f32[4,512]{1,0:T(4,128)S(1)} %dynamic-slice_bitcast_fusion.9, pred[512,2048]{1,0:T(8,128)(4,1)} %copy-done.1, bf16[2048,4,64]{0,2,1:T(8,128)(2,1)} %get-tuple-element.484, ...), kind=kOutput, calls=%fused_computation.18.clone.1 | convolution fusion | flops 557840384 | bytes 35930116 | tf_op jit(solution)/shard_map/while/body/eval_jaxpr/while/body/eval_jaxpr/qhd,khd->hqk/dot_general | solution.py:209
  473.2 11.0 %multiply_convert_fusion.14 = bf16[4,512,2048]{2,1,0:T(8,128)(2,1)} fusion(f32[4,512,2048]{2,1,0:T(8,128)} %get-tuple-element.425, f32[4,512,2048]{2,1,0:T(8,128)S(1)} %fusion.174, f32[4,512]{1,0:T(4,128)} %get-tuple-element.426, f32[4,512]{1,0:T(4,128)S(1)} %dynamic-slice_bitcast_fusion.9, pred[512,2048]{1,0:T(8,128)(4,1)} %copy-done.1), kind=kLoop, calls=%fused_computation.17.clone.1 | loop fusion | flops 25165824 | bytes 43008000 | tf_op jit(solution)/shard_map/while/body/eval_jaxpr/while/body/eval_jaxpr/convert_element_type | solution.py:213
  500.8 9.7 fusion.64
  521.7 9.5 fusion.65
  548.1 9.5 multiply_bitcast_fusion
  578.0 10.0 fusion.102
  624.2 14.7 %reduce-scatter.22.cloned.1.call-done = bf16[128,40]{1,0:T(8,128)(2,1)} async-done(((bf16[1024,40]{1,0:T(8,128)(2,1)}), bf16[128,40]{1,0:T(8,128)(2,1)}) %reduce-scatter.22.cloned.1.call-update) | async-done | bytes 10256
  640.3 63.9 %reduce-scatter.24.cloned.1.call-done = bf16[128,256]{1,0:T(8,128)(2,1)} async-done(((bf16[1024,256]{1,0:T(8,128)(2,1)}), bf16[128,256]{1,0:T(8,128)(2,1)}) %reduce-scatter.24.cloned.1.call-update) | async-done | bytes 65552
  705.8 65.7 %reduce-scatter.28.cloned.1.call-done = bf16[128,704]{1,0:T(8,128)(2,1)} async-done(((bf16[1024,704]{1,0:T(8,128)(2,1)}), bf16[128,704]{1,0:T(8,128)(2,1)}) %reduce-scatter.28.cloned.1.call-update) | async-done | bytes 180240
  773.3 85.2 %all-reduce.15.cloned.1.call-done = (bf16[1024,1024]{1,0:T(8,128)(2,1)}, bf16[1024,1024]{1,0:T(8,128)(2,1)}) async-done(((bf16[1024,1024]{1,0:T(8,128)(2,1)}, bf16[1024,1024]{1,0:T(8,128)(2,1)}), (bf16[1024,1024]{1,0:T(8,128)(2,1)}, bf16[1024,1024]{1,0:T(8,128)(2,1)})) %all-reduce.15.cloned.1.call-update) | async-done | bytes 4194320 | tf_op jit(solution)/shard_map/psum | solution.py:125
  864.0 41.2 %all-reduce.4 = (f32[1024]{0:T(1024)S(1)}, f32[1024]{0:T(1024)S(1)}) all-reduce(f32[1024]{0:T(1024)S(1)} %get-tuple-element.243, f32[1024]{0:T(1024)S(1)} %copy-done.61), channel_id=16, replica_groups=mesh['fsdp'=4,'ctx'=2,'tp'=4] {'fsdp','ctx','tp'}, use_global_device_ids=true, to_apply=%region_25.26.clone | all-reduce | flops 2048 | bytes 16384
  915.9 18.7 %reduce-scatter.26.cloned.1.call-done = bf16[128,1408]{1,0:T(8,128)(2,1)} async-done(((bf16[1024,1408]{1,0:T(8,128)(2,1)}), bf16[128,1408]{1,0:T(8,128)(2,1)}) %reduce-scatter.26.cloned.1.call-update) | async-done | bytes 360464
  937.5 136.8 %reduce-scatter.20.cloned.1.call-done = f32[32,640]{1,0:T(8,128)} async-done(((f32[1024,640]{1,0:T(8,128)}), f32[32,640]{1,0:T(8,128)}) %reduce-scatter.20.cloned.1.call-update) | async-done | bytes 81936 | tf_op jit(solution)/shard_map/reduce_scatter | solution.py:510
  (336 shorter events, 313.4 us)
Async XLA Ops:
  8.0 48.0 %copy-start.55 = (s32[1,2048]{1,0:T(1,128)S(1)}, s32[1,2048]{1,0:T(1,128)}, u32[]{:S(2)}) copy-start(s32[1,2048]{1,0:T(1,128)} %param.15) | copy-start | bytes 24580
  8.0 49.0 %copy-start.60 = (f32[1,128,40]{1,2,0:T(8,128)S(1)}, f32[1,128,40]{1,2,0:T(8,128)}, u32[]{:S(2)}) copy-start(f32[1,128,40]{1,2,0:T(8,128)} %param.17) | copy-start | bytes 61444
  8.0 49.0 %copy-start.54 = (f32[1,256,128]{2,1,0:T(8,128)S(1)}, f32[1,256,128]{2,1,0:T(8,128)}, u32[]{:S(2)}) copy-start(f32[1,256,128]{2,1,0:T(8,128)} %param.19) | copy-start | bytes 393220
  8.0 95.0 %all-gather.14.cloned.1.call-start = ((), (), s32[]{:S(2)}) async-start(), calls=%async_computation.13 | async-start | bytes 1351680 | tf_op jit(solution)/shard_map/all_gather | solution.py:81
  9.7 147.4 %all-gather.12.cloned.1.call-start = ((), (), s32[]{:S(2)}) async-start(), calls=%async_computation.7 | async-start | bytes 1572864 | tf_op jit(solution)/shard_map/all_gather | solution.py:272
  53.5 30.3 %copy-start.56 = (f32[1024]{0:T(1024)}, f32[1024]{0:T(1024)S(1)}, u32[]{:S(2)}) copy-start(f32[1024]{0:T(1024)S(1)} %convert_element_type.294) | copy-start | bytes 12292
  101.0 38.4 %copy-start.27 = (f32[1024,32]{0,1:T(8,128)}, f32[1024,32]{0,1:T(8,128)S(1)}, u32[]{:S(2)}) copy-start(f32[1024,32]{0,1:T(8,128)S(1)} %get-tuple-element.308) | copy-start | bytes 393220
  107.9 31.5 %copy-start.38 = (f32[1024,32]{0,1:T(8,128)S(1)}, f32[1024,32]{0,1:T(8,128)}, u32[]{:S(2)}) copy-start(f32[1024,32]{0,1:T(8,128)} %get-tuple-element.307) | copy-start | bytes 393220
  110.4 157.2 %all-reduce.11.cloned.1.call-start = ((), (), s32[]{:S(2)}) async-start(), calls=%async_computation.8 | async-start | bytes 4194304 | tf_op jit(solution)/shard_map/psum | solution.py:125
  215.2 63.9 %all-gather.16.cloned.1.call-start = ((), (), s32[]{:S(2)}) async-start(), calls=%async_computation.14 | async-start | bytes 3244032 | tf_op jit(solution)/shard_map/all_gather | solution.py:70
  217.2 105.9 %all-gather.18.cloned.1.call-start = ((), (), s32[]{:S(2)}) async-start(), calls=%async_computation.15 | async-start | bytes 1622016 | tf_op jit(solution)/shard_map/all_gather | solution.py:73
  217.9 169.7 %all-reduce.13.cloned.1.call-start = ((), (), s32[]{:S(2)}) async-start(), calls=%async_computation.9 | async-start | bytes 4194304 | tf_op jit(solution)/shard_map/psum | solution.py:129
  337.9 220.5 %reduce-scatter.16.cloned.1.call-start = ((), (), s32[]{:S(2)}) async-start(), calls=%async_computation.10 | async-start | bytes 98304 | tf_op jit(solution)/shard_map/reduce_scatter | solution.py:390
  500.8 9.7 copy-start.41
  540.8 51.0 %reduce-scatter.18.cloned.1.call-start = ((), (), s32[]{:S(2)}) async-start(), calls=%async_computation.11 | async-start | bytes 1572864 | tf_op jit(solution)/shard_map/reduce_scatter | solution.py:393
  547.2 91.7 %reduce-scatter.22.cloned.1.call-start = ((), (), s32[]{:S(2)}) async-start(), calls=%async_computation.16 | async-start | bytes 294912
  562.3 141.8 %reduce-scatter.24.cloned.1.call-start = ((), (), s32[]{:S(2)}) async-start(), calls=%async_computation.17 | async-start | bytes 589824
  566.3 205.1 %reduce-scatter.28.cloned.1.call-start = ((), (), s32[]{:S(2)}) async-start(), calls=%async_computation.19 | async-start | bytes 1769472
  572.7 285.8 %all-reduce.15.cloned.1.call-start = ((), (), s32[]{:S(2)}) async-start(), calls=%async_computation.20 | async-start | bytes 8388608 | tf_op jit(solution)/shard_map/psum | solution.py:125
  599.6 335.0 %reduce-scatter.26.cloned.1.call-start = ((), (), s32[]{:S(2)}) async-start(), calls=%async_computation.18 | async-start | bytes 3244032
  617.9 456.4 %reduce-scatter.20.cloned.1.call-start = ((), (), s32[]{:S(2)}) async-start(), calls=%async_computation.12 | async-start | bytes 2703360 | tf_op jit(solution)/shard_map/reduce_scatter | solution.py:510
  624.1 234.4 %copy-start.57 = (f32[1024]{0:T(1024)S(1)}, f32[1024]{0:T(1024)}, u32[]{:S(2)}) copy-start(f32[1024]{0:T(1024)} %copy-done.56) | copy-start | bytes 12292
  624.2 234.4 %copy-start.59 = (f32[1024]{0:T(1024)S(1)}, f32[1024]{0:T(1024)}, u32[]{:S(2)}) copy-start(f32[1024]{0:T(1024)} %copy-done.58) | copy-start | bytes 12292
  858.5 47.8 %copy-start.30 = (bf16[1024,1024]{1,0:T(8,128)(2,1)S(1)}, bf16[1024,1024]{1,0:T(8,128)(2,1)}, u32[]{:S(2)}) copy-start(bf16[1024,1024]{1,0:T(8,128)(2,1)} %get-tuple-element.283) | copy-start | bytes 6291460
  (64 other events, 263.9 us)
Sparse Core Ops, SparseCore 0:
  12.3 57.0 all-gather.13
  110.5 25.4 all-gather.11
  215.3 52.2 all-reduce.10
  338.0 49.6 all-reduce.12
  541.0 9.9 reduce-scatter.15
  553.0 20.3 reduce-scatter.17
  577.6 61.1 reduce-scatter.21
  643.2 60.9 reduce-scatter.23
  707.6 63.8 reduce-scatter.27
  773.9 84.5 all-reduce.14
  862.1 72.4 reduce-scatter.25
  937.3 136.9 reduce-scatter.19
Sparse Core Ops, SparseCore 1:
  218.5 60.5 all-gather.15
  281.7 41.3 all-gather.17
where the time goes:
time: 1090 us; the launch traced here: 1080 us
  waiting for transfers between devices  524 us (48%)
  matrix products  219 us (20%)
  blocking collectives  143 us (13%)
  local copies, waits for them, and re-layouts  89.8 us (8%)
  other arithmetic  87.9 us (8%)
  between operations  16.8 us (2%)
    unnamed x18, waiting for transfers between devices  163 us
    reduce_scatter x1, waiting for transfers between devices, shards(): lax.psum_scatter(shared_grads[0], ('fsdp', 'ctx', 'tp'), scatter_dimensio...  137 us
    psum x2, waiting for transfers between devices, branch_total(): lax.psum(partial_value.astype(jnp.bfloat16), 'tp').astype(jnp.float32)  135 us
    unnamed x2, blocking collectives  83.2 us
    psum x1, waiting for transfers between devices, grad_total(): lax.psum(partial_value.astype(jnp.bfloat16), 'tp').astype(jnp.float32)  49.7 us
    unnamed x132, local copies, waits for them, and re-layouts  44.9 us
    all_gather x1, waiting for transfers between devices, fetch_split(): lax.all_gather(w_down[layer_index].astype(jnp.bfloat16), ('fsdp', 'ctx'),...  35.3 us
    all_gather x1, blocking collectives, fetch_split(): lax.all_gather(w_out[layer_index].astype(jnp.bfloat16), ('fsdp', 'ctx'),...  28.9 us
  transfers between devices with their start and end apart: 14, of which 10 were waited for; matrix products, arithmetic and copies ran while one was open for 14% of the time, Pallas kernels for 0%

commit v1 on v0

v1 whole, which is shorter than its diff:
```python
import jax
import jax.numpy as jnp
from jax import lax
from jax.experimental import pallas as pl
from jax.experimental.pallas import tpu as pltpu
from jax.sharding import PartitionSpec as P

HEAD_DIM = 64
RANK_Q = 6
RANK_KV = 2
RANKS = 10
KV = 2 * RANK_KV
MOST_DOC = 768
EPSILON = 1e-05
LANES = 128
BF16 = jnp.bfloat16
F32 = jnp.float32
MASKED = -1e30


def inverse_rms(values):
    return lax.rsqrt(jnp.mean(values * values, axis=-1, keepdims=True) + EPSILON)


def norm_back(grad_value, values, inverse, gain):
    scaled = grad_value * gain
    normal = values * inverse
    return inverse * (scaled - normal * jnp.mean(scaled * normal, axis=-1, keepdims=True))


def dot(left, right, dims):
    return lax.dot_general(left, right, (dims, ((), ())), preferred_element_type=F32)


def shift(value, axes, size, step):
    return lax.ppermute(value, axes, [(i, (i + step) % size) for i in range(size)])


def swap(value, axis, size, bit):
    return lax.ppermute(value, axis, [(i, i ^ bit) for i in range(size)])


def gather_direct(value, axis, size):
    me = lax.axis_index(axis)
    parts = [(me, value)]
    for step in range(1, size):
        parts.append(((me - step) % size, shift(value, axis, size, step)))
    out = jnp.zeros((size,) + value.shape, value.dtype)
    for place, part in parts:
        out = lax.dynamic_update_slice(out, part[None], (place,) + (0,) * value.ndim)
    return out


def gather_pair(value, axis, size, bit):
    mine = (lax.axis_index(axis) // bit) % 2 == 0
    other = swap(value, axis, size, bit)
    return jnp.stack([jnp.where(mine, value, other), jnp.where(mine, other, value)])


def take(value, index):
    return lax.dynamic_index_in_dim(value, index, 0, keepdims=False)


def scatter_direct(value, axis, size):
    me = lax.axis_index(axis)
    got = [
        shift(take(value, (me + step) % size), axis, size, step) for step in range(1, size)
    ]
    total = take(value, me).astype(F32)
    for part in got:
        total = total + part.astype(F32)
    return total


def scatter_pair(value, axis, size, bit):
    mine = (lax.axis_index(axis) // bit) % 2
    got = swap(take(value, 1 - mine).astype(BF16), axis, size, bit)
    return take(value, mine).astype(F32) + got.astype(F32)


def attention_mask(first_ref, window, block):
    start = first_ref[...]
    place = lax.broadcasted_iota(jnp.int32, (window, block), 0)
    query_place = lax.broadcasted_iota(jnp.int32, (window, block), 1) + (window - block)
    return jnp.where((place >= start) & (place <= query_place), 0.0, MASKED)


def head_rows(wa_ref, wide_ref, head):
    factors = wa_ref[head].astype(F32)
    key_rows = (factors[0:1] * wide_ref[0] + factors[1:2] * wide_ref[1]) * (1.0 / RANK_KV)
    value_rows = (factors[2:3] * wide_ref[2] + factors[3:4] * wide_ref[3]) * (1.0 / RANK_KV)
    return factors, key_rows.astype(BF16), value_rows.astype(BF16)


def forward_kernel(
    first_ref, a_ref, bq_ref, wa_ref, wb_ref, mixed_ref, lse_ref, q_ref, bias_ref, wide_ref, s_ref
):
    heads = a_ref.shape[0]
    window, block = bias_ref.shape
    bias_ref[...] = attention_mask(first_ref, window, block)
    wide_ref[...] = wb_ref[...].astype(F32)
    spans = [pl.ds(j * block, block) for j in range(window // block)]

    def one_head(head, carry):
        factors = a_ref[head]
        query = factors[0:1] * bq_ref[0]
        for r in range(1, RANK_Q):
            query = query + factors[r : r + 1] * bq_ref[r]
        query = (query * (1.0 / RANK_Q)).astype(BF16) * jnp.asarray(HEAD_DIM**-0.5, BF16)
        q_ref[head] = query
        _, key_rows, value_rows = head_rows(wa_ref, wide_ref, head)
        top = jnp.full((1, block), MASKED, F32)
        for j, span in enumerate(spans):
            keys = key_rows[:, j * block : (j + 1) * block]
            scores = dot(keys, query, ((0,), (0,))) + bias_ref[span, :]
            s_ref[span, :] = scores
            top = jnp.maximum(top, jnp.max(scores, axis=0, keepdims=True))
        total = jnp.zeros((1, block), F32)
        for span in spans:
            weight = jnp.exp(s_ref[span, :] - top)
            s_ref[span, :] = weight
            total = total + jnp.sum(weight, axis=0, keepdims=True)
        lse_ref[head] = top + jnp.log(total)
        scale = 1.0 / total
        mixed = jnp.zeros((HEAD_DIM, block), F32)
        for j, span in enumerate(spans):
            probs = (s_ref[span, :] * scale).astype(BF16)
            mixed = mixed + dot(
                value_rows[:, j * block : (j + 1) * block], probs, ((1,), (0,))
            )
        mixed_ref[head] = mixed.astype(BF16)
        return carry

    lax.fori_loop(0, heads, one_head, 0)


def backward_kernel(
    first_ref,
    a_ref,
    bq_ref,
    wa_ref,
    wb_ref,
    lse_ref,
    q_ref,
    go_ref,
    ga_ref,
    gbq_ref,
    gwa_ref,
    gwb_ref,
    bias_ref,
    wide_ref,
    p_ref,
    dp_ref,
):
    heads = a_ref.shape[0]
    window, block = bias_ref.shape
    bias_ref[...] = attention_mask(first_ref, window, block)
    wide_ref[...] = wb_ref[...].astype(F32)
    gbq_ref[...] = jnp.zeros_like(gbq_ref)
    gwb_ref[...] = jnp.zeros_like(gwb_ref)
    count = window // block
    spans = [pl.ds(j * block, block) for j in range(count)]

    def one_head(head, carry):
        factors, key_rows, value_rows = head_rows(wa_ref, wide_ref, head)
        query = q_ref[head]
        grad_out = go_ref[head]
        lse = lse_ref[head]
        inner = jnp.zeros((1, block), F32)
        for j, span in enumerate(spans):
            cut = slice(j * block, (j + 1) * block)
            scores = dot(key_rows[:, cut], query, ((0,), (0,))) + bias_ref[span, :]
            probs = jnp.exp(scores - lse)
            grad_probs = dot(value_rows[:, cut], grad_out, ((0,), (0,)))
            p_ref[span, :] = probs
            dp_ref[span, :] = grad_probs
            inner = inner + jnp.sum(probs * grad_probs, axis=0, keepdims=True)
        grad_query = jnp.zeros((HEAD_DIM, block), F32)
        for j, span in enumerate(spans):
            cut = slice(j * block, (j + 1) * block)
            probs = p_ref[span, :]
            grad_scores = (probs * (dp_ref[span, :] - inner)).astype(BF16)
            grad_query = grad_query + dot(key_rows[:, cut], grad_scores, ((1,), (0,)))
            grad_keys = dot(query, grad_scores, ((1,), (1,))) * (1.0 / RANK_KV)
            grad_values = dot(grad_out, probs.astype(BF16), ((1,), (1,))) * (1.0 / RANK_KV)
            rows = []
            for r in range(KV):
                grad = grad_keys if r < RANK_KV else grad_values
                rows.append(jnp.sum(grad * wide_ref[r, :, span], axis=0, keepdims=True))
                gwb_ref[r, :, span] += factors[r : r + 1, cut] * grad
            gwa_ref[head, :, span] = jnp.concatenate(rows, axis=0)
        grad_query = grad_query * (HEAD_DIM**-0.5 / RANK_Q)
        own = a_ref[head]
        rows = []
        for r in range(RANK_Q):
            rows.append(jnp.sum(grad_query * bq_ref[r], axis=0, keepdims=True))
            gbq_ref[r] += own[r : r + 1] * grad_query
        ga_ref[head] = jnp.concatenate(rows, axis=0)
        return carry

    lax.fori_loop(0, heads, one_head, 0)


VMEM_LIMIT = 56 * 1024 * 1024


def whole_specs(count):
    return [pl.BlockSpec(memory_space=pltpu.VMEM)] * count


def attend_forward(first, a_rows, b_query, win_a, win_b):
    heads, _, block = a_rows.shape
    window = win_a.shape[-1]
    return pl.pallas_call(
        forward_kernel,
        out_shape=(
            jax.ShapeDtypeStruct((heads, HEAD_DIM, block), BF16),
            jax.ShapeDtypeStruct((heads, 1, block), F32),
            jax.ShapeDtypeStruct((heads, HEAD_DIM, block), BF16),
        ),
        in_specs=whole_specs(5),
        out_specs=tuple(whole_specs(3)),
        scratch_shapes=[
            pltpu.VMEM((window, block), F32),
            pltpu.VMEM((KV, HEAD_DIM, window), F32),
            pltpu.VMEM((window, block), F32),
        ],
        compiler_params=pltpu.CompilerParams(vmem_limit_bytes=VMEM_LIMIT),
        name="attend_forward",
    )(first, a_rows, b_query, win_a, win_b)


def attend_backward(first, a_rows, b_query, win_a, win_b, lse, query, grad_mixed):
    heads, _, block = a_rows.shape
    window = win_a.shape[-1]
    return pl.pallas_call(
        backward_kernel,
        out_shape=(
            jax.ShapeDtypeStruct((heads, RANK_Q, block), F32),
            jax.ShapeDtypeStruct((RANK_Q, HEAD_DIM, block), F32),
            jax.ShapeDtypeStruct((heads, KV, window), F32),
            jax.ShapeDtypeStruct((KV, HEAD_DIM, window), F32),
        ),
        in_specs=whole_specs(8),
        out_specs=tuple(whole_specs(4)),
        scratch_shapes=[
            pltpu.VMEM((window, block), F32),
            pltpu.VMEM((KV, HEAD_DIM, window), F32),
            pltpu.VMEM((window, block), F32),
            pltpu.VMEM((window, block), F32),
        ],
        compiler_params=pltpu.CompilerParams(vmem_limit_bytes=VMEM_LIMIT),
        name="attend_backward",
    )(first, a_rows, b_query, win_a, win_b, lse, query, grad_mixed)


def rotate(rows, cosine, sine):
    half = HEAD_DIM // 2
    lower, upper = rows[:, :half], rows[:, half:]
    return jnp.concatenate(
        [lower * cosine - upper * sine, lower * sine + upper * cosine], axis=1
    )


def make_shards(mesh):
    n_f, n_c, n_tp = mesh.shape["fsdp"], mesh.shape["ctx"], mesh.shape["tp"]
    n_hi, n_lo = 2, n_tp // 2

    def shards(
        resid_in,
        segment_ids,
        cotangent,
        w_factor_a,
        w_factor_b,
        w_out,
        w_gate_up,
        w_down,
        attn_gains,
        ffn_gains,
    ):
        seq_count, local_len, width = resid_in.shape
        assert seq_count == 1 and w_factor_a.shape[0] == 1 and n_lo == 2
        full_len = segment_ids.shape[1]
        block = local_len // n_tp
        extra = -(-(MOST_DOC - 1) // block)
        window = (extra + 1) * block
        a_cols = w_factor_a.shape[2]
        heads = n_tp * a_cols // RANKS
        b_cols = w_factor_b.shape[2]
        b_rows = w_factor_b.shape[1]
        b_parts = b_cols // LANES
        fc_cols = w_down.shape[2]
        hidden = w_down.shape[1]
        o_rows = w_out.shape[1]

        f_index, c_index, t_index = (
            lax.axis_index("fsdp"),
            lax.axis_index("ctx"),
            lax.axis_index("tp"),
        )
        hi, lo = t_index // 2, t_index % 2
        place = c_index * n_tp + t_index
        n_place = n_c * n_tp

        gains = jnp.concatenate([attn_gains, ffn_gains], axis=1).astype(BF16)
        gain_count = gains.shape[1]
        gain_rows = 16 * (-(-gain_count // (16 * LANES)))
        gains = jnp.pad(gains.reshape(-1), (0, gain_rows * LANES - gain_count))
        b_shard = w_factor_b[0].astype(BF16).reshape(b_rows, b_parts, LANES)
        a_shard = w_factor_a[0].astype(BF16).T
        pack = jnp.concatenate(
            [
                b_shard.transpose(1, 0, 2).reshape(-1, LANES),
                a_shard.reshape(-1, LANES),
                gains.reshape(-1, LANES),
            ],
            axis=0,
        )
        n_b = b_parts * b_rows
        n_a = a_cols * fc_cols // LANES
        pack = gather_direct(pack, "fsdp", n_f)
        after_pack = pack
        pack = gather_pair(pack, "ctx", n_c, 1)
        pack = gather_pair(pack, "tp", n_tp, 2)
        pack = gather_pair(pack, "tp", n_tp, 1)
        pack = pack.transpose(3, 2, 1, 0, 4, 5)
        weight_b = pack[:, :, :, :, :n_b].reshape(-1, b_parts, b_rows, LANES)
        weight_b = weight_b.transpose(0, 2, 1, 3).reshape(width, b_cols)
        weight_a = pack[:, :, :, :, n_b : n_b + n_a].reshape(n_f, n_c, n_tp, a_cols, fc_cols)
        weight_a = weight_a.transpose(2, 3, 0, 1, 4).reshape(n_tp * a_cols, width)
        gains_all = pack[:, :, :, :, n_b + n_a :].reshape(-1, gain_rows * LANES)[:, :gain_count]
        gains_all = gains_all.reshape(-1, 2, gain_count // 2).transpose(1, 0, 2)
        gains_all = gains_all.reshape(2, width).astype(F32)
        gain_attn, gain_ffn = gains_all[0:1], gains_all[1:2]

        big = jnp.concatenate(
            [
                w_gate_up[0, 0].astype(BF16).T,
                w_gate_up[0, 1].astype(BF16).T,
                w_down[0].astype(BF16),
                w_out[0].astype(BF16),
            ],
            axis=0,
        )
        big, _ = lax.optimization_barrier((big, after_pack))
        big = gather_direct(big, "fsdp", n_f)
        big = gather_pair(big, "ctx", n_c, 1)
        big = big.transpose(2, 1, 0, 3).reshape(-1, width)
        weight_g = big[:hidden]
        weight_u = big[hidden : 2 * hidden]
        weight_d = big[2 * hidden : 3 * hidden]
        weight_o = gather_pair(big[3 * hidden :], "tp", n_tp, 2)
        weight_o = gather_pair(weight_o, "tp", n_tp, 1)
        weight_o = weight_o.transpose(1, 0, 2, 3).reshape(n_tp * o_rows, width)

        seg_here = lax.dynamic_slice_in_dim(segment_ids[0], place * block, block, 0)
        first = jnp.sum((segment_ids[0][:, None] < seg_here[None, :]).astype(jnp.int32), axis=0)
        token = place * block + jnp.arange(block, dtype=jnp.int32)
        position = (token - first).astype(F32)
        first = (first - place * block + extra * block).reshape(1, block)
        frequency = 10000.0 ** (
            -2.0 * jnp.arange(HEAD_DIM // 2, dtype=F32) / HEAD_DIM
        )
        angles = frequency[:, None] * position[None, :]
        cosine, sine = jnp.cos(angles)[None], jnp.sin(angles)[None]

        stream = resid_in[0].reshape(n_tp, block, width)
        own = take(stream, t_index)
        inverse_attn = inverse_rms(own)
        normed = (own * inverse_attn * gain_attn).astype(BF16)
        a_rows = dot(weight_a, normed, ((1,), (1,))).reshape(heads, RANKS, block)
        b_raw = dot(weight_b, normed, ((0,), (1,))).reshape(RANKS, HEAD_DIM, block)
        b_rot = rotate(b_raw[: RANK_Q + RANK_KV], cosine, sine)
        b_query = b_rot[:RANK_Q]
        b_kv = jnp.concatenate([b_rot[RANK_Q:], b_raw[RANK_Q + RANK_KV :]], axis=0)
        payload = jnp.concatenate(
            [
                b_kv.reshape(KV * HEAD_DIM, block),
                a_rows[:, RANK_Q:].reshape(heads * KV, block),
            ],
            axis=0,
        ).astype(BF16)
        around = [
            lax.ppermute(
                payload, ("ctx", "tp"), [(i, i + step) for i in range(n_place - step)]
            )
            for step in range(extra, 0, -1)
        ]
        win = jnp.concatenate(around + [payload], axis=1)
        win_b = win[: KV * HEAD_DIM].reshape(KV, HEAD_DIM, window)
        win_a = win[KV * HEAD_DIM :].reshape(heads, KV, window)

        mixed, lse, query = attend_forward(first, a_rows, b_query, win_a, win_b)
        mixed = mixed.reshape(heads * HEAD_DIM, block)
        attn_out = dot(mixed, weight_o, ((0,), (0,)))
        mid = own + attn_out
        inverse_ffn = inverse_rms(mid)
        normed_ffn = (mid * inverse_ffn * gain_ffn).astype(BF16)

        near_rows = gather_pair(normed_ffn, "tp", n_tp, 1)
        far_rows = gather_pair(swap(normed_ffn, "tp", n_tp, 2), "tp", n_tp, 1)
        grad_all = cotangent[0].reshape(n_hi, n_lo * block, width)

        def half(rows, grad_rows):
            rows = rows.reshape(n_lo * block, width)
            gate = dot(rows, weight_g, ((1,), (1,)))
            up = dot(rows, weight_u, ((1,), (1,)))
            grad_act = dot(grad_rows, weight_d, ((1,), (1,)))
            squash = jax.nn.sigmoid(gate)
            act = (gate * squash * up).astype(BF16)
            grad_gate = (grad_act * up * squash * (1.0 + gate * (1.0 - squash))).astype(BF16)
            grad_up = (grad_act * gate * squash).astype(BF16)
            back = dot(grad_gate, weight_g, ((1,), (0,))) + dot(grad_up, weight_u, ((1,), (0,)))
            ahead = dot(act, weight_d, ((1,), (0,)))
            both = lambda v: v.reshape(n_lo, block, width)
            return rows, act, grad_gate, grad_up, both(back), both(ahead)

        grad_near = take(grad_all, hi).astype(BF16)
        grad_far = take(grad_all, 1 - hi).astype(BF16)
        near = half(near_rows, grad_near)
        far = half(far_rows, grad_far)
        back_far = scatter_pair(far[4], "tp", n_tp, 1).astype(BF16)
        back_far = swap(back_far, "tp", n_tp, 2)
        grad_normed_ffn = scatter_pair(near[4], "tp", n_tp, 1) + back_far.astype(F32)
        ahead_far = scatter_pair(far[5], "tp", n_tp, 1).astype(BF16)
        ahead_far = swap(ahead_far, "tp", n_tp, 2)
        ffn_out = scatter_pair(near[5], "tp", n_tp, 1) + ahead_far.astype(F32)

        def spread(value):
            beside = swap(value, "tp", n_tp, 1)
            across = swap(value, "tp", n_tp, 2)
            diagonal = swap(across, "tp", n_tp, 1)
            out = jnp.zeros((n_tp,) + value.shape, value.dtype)
            for bit, part in enumerate((value, beside, across, diagonal)):
                out = lax.dynamic_update_slice(out, part[None], (t_index ^ bit, 0, 0))
            return out.reshape(local_len, width).astype(F32)

        block_out = resid_in + spread((attn_out + ffn_out).astype(BF16))[None]

        def columns(value, which):
            value = value.reshape(value.shape[0], n_f, n_c, fc_cols)
            value = lax.dynamic_index_in_dim(value, which, 2, keepdims=False)
            return value.reshape(value.shape[0], n_f * fc_cols)

        rows_all = jnp.concatenate([near[0], far[0]], axis=0)
        act_all = jnp.concatenate([near[1], far[1]], axis=0)
        gate_all = jnp.concatenate([near[2], far[2]], axis=0)
        up_all = jnp.concatenate([near[3], far[3]], axis=0)
        cot_all = jnp.concatenate([grad_near, grad_far], axis=0)

        def big_grads(which):
            rows_cut = columns(rows_all, which)
            cot_cut = columns(cot_all, which)
            return jnp.concatenate(
                [
                    dot(gate_all, rows_cut, ((0,), (0,))),
                    dot(up_all, rows_cut, ((0,), (0,))),
                    dot(act_all, cot_cut, ((0,), (0,))),
                ],
                axis=0,
            )

        def over_fc(send, keep):
            total = keep + swap(send.astype(BF16), "ctx", n_c, 1).astype(F32)
            total = total.astype(BF16).reshape(-1, n_f, fc_cols).transpose(1, 0, 2)
            return scatter_direct(total, "fsdp", n_f)

        grad_big = over_fc(big_grads(1 - c_index), big_grads(c_index))
        grad_gate_w = grad_big[:hidden].T
        grad_up_w = grad_big[hidden : 2 * hidden].T
        grad_down_w = grad_big[2 * hidden :]

        own_cot = take(cotangent[0].reshape(n_tp, block, width), t_index)
        gain_grad_ffn = jnp.sum(grad_normed_ffn * mid * inverse_ffn, axis=0)
        delta_mid = norm_back(grad_normed_ffn, mid, inverse_ffn, gain_ffn)
        grad_attn = (own_cot + delta_mid).astype(BF16)
        grad_out = dot(mixed, grad_attn, ((1,), (0,))).reshape(n_hi, n_lo, o_rows, width)
        grad_out = scatter_pair(grad_out.transpose(1, 0, 2, 3), "tp", n_tp, 1)
        grad_out = scatter_pair(grad_out, "tp", n_tp, 2)
        grad_out = over_fc(columns(grad_out, 1 - c_index), columns(grad_out, c_index))

        grad_mixed = dot(weight_o, grad_attn, ((1,), (1,))).astype(BF16)
        ga_q, gb_q, gw_a, gw_b = attend_backward(
            first,
            a_rows,
            b_query,
            win_a,
            win_b,
            lse,
            query,
            grad_mixed.reshape(heads, HEAD_DIM, block),
        )
        gw = jnp.concatenate(
            [gw_b.reshape(KV * HEAD_DIM, window), gw_a.reshape(heads * KV, window)], axis=0
        )
        total = gw[:, extra * block :]
        for step in range(1, extra + 1):
            part = gw[:, (extra - step) * block : (extra - step + 1) * block].astype(BF16)
            part = lax.ppermute(
                part, ("ctx", "tp"), [(i + step, i) for i in range(n_place - step)]
            )
            total = total + part.astype(F32)
        gb_kv = total[: KV * HEAD_DIM].reshape(KV, HEAD_DIM, block)
        ga_kv = total[KV * HEAD_DIM :].reshape(heads, KV, block)
        grad_b = jnp.concatenate(
            [
                rotate(jnp.concatenate([gb_q, gb_kv[:RANK_KV]], axis=0), cosine, -sine),
                gb_kv[RANK_KV:],
            ],
            axis=0,
        )
        grad_b = grad_b.reshape(b_cols, block).astype(BF16)
        grad_a = jnp.concatenate([ga_q, ga_kv], axis=1).reshape(heads * RANKS, block).astype(BF16)
        grad_normed = dot(grad_a, weight_a, ((0,), (0,))) + dot(grad_b, weight_b, ((0,), (1,)))
        gain_grad_attn = jnp.sum(grad_normed * own * inverse_attn, axis=0)
        delta = delta_mid + norm_back(grad_normed, own, inverse_attn, gain_attn)
        resid_grad = cotangent + spread(delta.astype(BF16))[None]

        grad_wa = dot(grad_a, normed, ((1,), (0,))).astype(BF16)
        grad_wa = grad_wa.reshape(n_hi, n_lo, a_cols, n_f, n_c, fc_cols)
        grad_wa = grad_wa.transpose(1, 0, 4, 3, 2, 5).reshape(n_lo, n_hi, n_c, n_f, n_a, LANES)
        grad_wb = jnp.einsum(
            "pkt,td->pdk",
            grad_b.reshape(b_parts, LANES, block),
            normed,
            preferred_element_type=F32,
        ).astype(BF16)
        grad_wb = grad_wb.reshape(b_parts, n_f, n_c, n_hi, n_lo, b_rows, LANES)
        grad_wb = grad_wb.transpose(4, 3, 2, 1, 0, 5, 6)
        grad_wb = grad_wb.reshape(n_lo, n_hi, n_c, n_f, n_b, LANES)
        gain_grads = jnp.stack([gain_grad_attn, gain_grad_ffn]).astype(BF16)
        gain_grads = gain_grads.reshape(2, n_f, n_c, n_hi, n_lo, gain_count // 2)
        gain_grads = gain_grads.transpose(4, 3, 2, 1, 0, 5).reshape(
            n_lo, n_hi, n_c, n_f, gain_count
        )
        gain_grads = jnp.pad(
            gain_grads, [(0, 0)] * 4 + [(0, gain_rows * LANES - gain_count)]
        ).reshape(n_lo, n_hi, n_c, n_f, gain_rows, LANES)
        pack = jnp.concatenate([grad_wb, grad_wa, gain_grads], axis=4)
        pack = scatter_pair(pack, "tp", n_tp, 1)
        pack = scatter_pair(pack, "tp", n_tp, 2)
        pack = scatter_pair(pack, "ctx", n_c, 1).astype(BF16)
        pack = scatter_direct(pack, "fsdp", n_f)
        part_b = pack[:n_b].reshape(b_parts, b_rows, LANES).transpose(1, 0, 2)
        part_b = part_b.reshape(1, b_rows, b_cols)
        part_a = pack[n_b : n_b + n_a].reshape(a_cols, fc_cols).T[None]
        part_gain = pack[n_b + n_a :].reshape(-1)[:gain_count].reshape(2, 1, gain_count // 2)
        return (
            block_out,
            resid_grad,
            part_a,
            part_b,
            grad_out[None],
            jnp.stack([grad_gate_w, grad_up_w])[None],
            grad_down_w[None],
            part_gain[0],
            part_gain[1],
        )

    return shards


def solution(mesh):
    return jax.shard_map(
        make_shards(mesh),
        mesh=mesh,
        in_specs=(
            P("fsdp", "ctx", None),
            P("fsdp", None),
            P("fsdp", "ctx", None),
            P(None, ("fsdp", "ctx"), "tp"),
            P(None, ("fsdp", "ctx", "tp"), None),
            P(None, "tp", ("fsdp", "ctx")),
            P(None, None, ("fsdp", "ctx"), "tp"),
            P(None, "tp", ("fsdp", "ctx")),
            P(None, ("fsdp", "ctx", "tp")),
            P(None, ("fsdp", "ctx", "tp")),
        ),
        out_specs=(
            P("fsdp", "ctx", None),
            P("fsdp", "ctx", None),
            P(None, ("fsdp", "ctx"), "tp"),
            P(None, ("fsdp", "ctx", "tp"), None),
            P(None, "tp", ("fsdp", "ctx")),
            P(None, None, ("fsdp", "ctx"), "tp"),
            P(None, "tp", ("fsdp", "ctx")),
            P(None, ("fsdp", "ctx", "tp")),
            P(None, ("fsdp", "ctx", "tp")),
        ),
        check_vma=False,
    )
```

time: 1090 us -> 496 us (0.46)
  waiting for transfers between devices: 524 us -> 154 us
  matrix products: 219 us -> 43.7 us
  blocking collectives: 143 us -> 0 us
  starting transfers between devices: 1.34 us -> 83.5 us
  Pallas kernels: 0 us -> 38.4 us
  other arithmetic: 87.9 us -> 61.1 us
  between operations: 16.8 us -> 2.55 us
  local copies, waits for them, and re-layouts: 89.8 us -> 104 us
    psum x3 -> x0, waiting for transfers between devices: 184 us -> none  [the longest x2 135 us: branch_total(): lax.psum(partial_value.astype(jnp.bfloat16), 'tp').astype(jnp.float32)]
    dot_general x41 -> x27, matrix products: 219 us -> 43.7 us  [the longest x26 43.1 us: dot(): lax.dot_general(left, right, (dims, ((), ())), preferred_element_type=F32)]
    unnamed x18 -> x0, waiting for transfers between devices: 163 us -> none
    ppermute x0 -> x49, waiting for transfers between devices: none -> 154 us  [the longest x28 98.7 us: swap(): return lax.ppermute(value, axis, [(i, i ^ bit) for i in range(size)])]
    reduce_scatter x3 -> x0, waiting for transfers between devices: 137 us -> none  [the longest x1 137 us: shards(): lax.psum_scatter(shared_grads[0], ('fsdp', 'ctx', 'tp'), scatter_dimensio...]
    ppermute x0 -> x49, starting transfers between devices: none -> 83.5 us  [the longest x15 46.7 us: shift(): lax.ppermute(value, axes, [(i, (i + step) % size) for i in range(size)])]
    unnamed x2 -> x0, blocking collectives: 83.2 us -> none
    all_gather x3 -> x0, blocking collectives: 59.5 us -> none  [the longest x1 28.9 us: fetch_split(): lax.all_gather(w_out[layer_index].astype(jnp.bfloat16), ('fsdp', 'ctx'),...]
  transfers between devices with their start and end apart: 14 -> 49, of which waited for: 10 -> 17; matrix products, arithmetic and copies ran while one was open for 14% -> 37% of each run, Pallas kernels for 0% -> 8%
where the time goes in v1:
time: 496 us; the launch traced here: 487 us
  waiting for transfers between devices  154 us (31%)
  local copies, waits for them, and re-layouts  104 us (21%)
  starting transfers between devices  83.5 us (17%)
  other arithmetic  61.1 us (12%)
  matrix products  43.7 us (9%)
  Pallas kernels  38.4 us (8%)
    ppermute x28, waiting for transfers between devices, swap(): return lax.ppermute(value, axis, [(i, i ^ bit) for i in range(size)])  98.7 us
    ppermute x15, waiting for transfers between devices, shift(): lax.ppermute(value, axes, [(i, (i + step) % size) for i in range(size)])  54.5 us
    ppermute x15, starting transfers between devices, shift(): lax.ppermute(value, axes, [(i, (i + step) % size) for i in range(size)])  46.7 us
    dot_general x26, matrix products, dot(): lax.dot_general(left, right, (dims, ((), ())), preferred_element_type=F32)  43.1 us
    ppermute x28, starting transfers between devices, swap(): return lax.ppermute(value, axis, [(i, i ^ bit) for i in range(size)])  22.6 us
    pallas_call x1, Pallas kernels, attend_backward(): pl.pallas_call(backward_kernel, out_shape=(jax.ShapeDtypeStruct((heads, R...  22.5 us
    pallas_call x1, Pallas kernels, attend_forward(): pl.pallas_call(forward_kernel, out_shape=(jax.ShapeDtypeStruct((heads, HE...  15.9 us
    unnamed x163, local copies, waits for them, and re-layouts  15.4 us
  transfers between devices with their start and end apart: 49, of which 17 were waited for; matrix products, arithmetic and copies ran while one was open for 37% of the time, Pallas kernels for 8%

profile of v1, /device:TPU:0, one launch (start us, length us, event | category | flops | bytes accessed | tf_op | source)
XLA Modules:
  0.0 487.2 jit_solution(148602266621006014)
XLA Ops:
  3.2 3.0 collective-permute-start
  30.4 3.2 collective-permute-done.3
  36.2 6.1 %collective-permute-done.9 = bf16[2368,128]{1,0:T(8,128)(2,1)S(1)} collective-permute-done((bf16[2368,128]{1,0:T(8,128)(2,1)}, bf16[2368,128]{1,0:T(8,128)(2,1)S(1)}, u32[]{:S(2)}, u32[]{:S(2)}) %collective-permute-start.9) | collective-permute-done | bytes 606240 | tf_op jit(solution)/shard_map/ppermute | solution.py:36
  42.4 24.0 %collective-permute-done.10 = bf16[2368,128]{1,0:T(8,128)(2,1)S(1)} collective-permute-done((bf16[2368,128]{1,0:T(8,128)(2,1)}, bf16[2368,128]{1,0:T(8,128)(2,1)S(1)}, u32[]{:S(2)}, u32[]{:S(2)}) %collective-permute-start.10) | collective-permute-done | bytes 606240 | tf_op jit(solution)/shard_map/ppermute | solution.py:36
  83.9 36.1 %collective-permute-done.12 = bf16[4,2368,128]{2,1,0:T(8,128)(2,1)} collective-permute-done((bf16[4,2368,128]{2,1,0:T(8,128)(2,1)S(1)}, bf16[4,2368,128]{2,1,0:T(8,128)(2,1)}, u32[]{:S(2)}, u32[]{:S(2)}) %collective-permute-start.12) | collective-permute-done | bytes 2424864 | tf_op jit(solution)/shard_map/ppermute | solution.py:40
  129.3 9.3 %collective-permute-done.13 = bf16[256,1024]{0,1:T(8,128)(2,1)S(1)} collective-permute-done((bf16[256,1024]{0,1:T(8,128)(2,1)S(1)}, bf16[256,1024]{0,1:T(8,128)(2,1)S(1)}, u32[]{:S(2)}, u32[]{:S(2)}) %collective-permute-start.13) | collective-permute-done | bytes 524320 | tf_op jit(solution)/shard_map/ppermute | solution.py:40
  142.9 4.2 collective-permute-start.6
  147.2 4.0 collective-permute-start.7
  162.5 15.9 %attend_forward.1 = (bf16[16,64,256]{2,1,0:T(8,128)(2,1)}, f32[16,1,256]{2,1,0:T(1,128)}, bf16[16,64,256]{2,1,0:T(8,128)(2,1)}) custom-call(s32[1,256]{1,0:T(1,128)} %bitcast.439, f32[16,10,256]{2,1,0:T(8,128)} %copy-done.32, f32[6,64,256]{2,1,0:T(8,128)} %fusion.53.bq_ref, bf16[16,4,1024]{2,1,0:T(4,128)(2,1)} %reshape.516.wa_ref, bf16[4,64,1024]{2,1,0:T(8,128)(2,1)} %bitcast.393), custom_call_target="tpu_custom_call" | custom-call | tf_op jit(solution)/shard_map/attend_forward/pallas_call | solution.py:214
  178.3 4.2 fusion.81
  201.7 3.6 multiply_reduce_fusion.3
  222.2 3.4 convolution_add_fusion.1
  234.6 3.8 copy.151
  262.2 10.3 %collective-permute-done.20 = bf16[256,1024]{1,0:T(8,128)(2,1)S(1)} collective-permute-done((bf16[256,1024]{1,0:T(8,128)(2,1)S(1)}, bf16[256,1024]{1,0:T(8,128)(2,1)S(1)}, u32[]{:S(2)}, u32[]{:S(2)}) %collective-permute-start.20) | collective-permute-done | bytes 524320 | tf_op jit(solution)/shard_map/ppermute | solution.py:40
  276.1 7.7 %collective-permute-done.26 = bf16[256,1024]{1,0:T(8,128)(2,1)S(1)} collective-permute-done((bf16[256,1024]{1,0:T(8,128)(2,1)S(1)}, bf16[256,1024]{1,0:T(8,128)(2,1)S(1)}, u32[]{:S(2)}, u32[]{:S(2)}) %collective-permute-start.26) | collective-permute-done | bytes 524320 | tf_op jit(solution)/shard_map/ppermute | solution.py:40
  289.4 22.5 %attend_backward.1 = (f32[16,6,256]{2,1,0:T(8,128)}, f32[6,64,256]{2,1,0:T(8,128)}, f32[16,4,1024]{2,1,0:T(4,128)}, f32[4,64,1024]{2,1,0:T(8,128)}) custom-call(s32[1,256]{1,0:T(1,128)} %bitcast.440, f32[16,10,256]{2,1,0:T(8,128)} %copy-done.32, f32[6,64,256]{2,1,0:T(8,128)} %fusion.53.bq_ref, bf16[16,4,1024]{2,1,0:T(4,128)(2,1)} %reshape.516.wa_ref, ...), custom_call_target="tpu_custom_call" | custom-call | tf_op jit(solution)/shard_map/attend_backward/pallas_call | solution.py:236
  347.8 3.8 collective-permute-done.31
  364.0 28.2 %collective-permute-done.45 = bf16[2112,512]{1,0:T(8,128)(2,1)S(1)} collective-permute-done((bf16[2112,512]{1,0:T(8,128)(2,1)S(1)}, bf16[2112,512]{1,0:T(8,128)(2,1)S(1)}, u32[]{:S(2)}, u32[]{:S(2)}) %collective-permute-start.45) | collective-permute-done | bytes 2162720 | tf_op jit(solution)/shard_map/ppermute | solution.py:40
  394.4 3.9 reshape.543
  398.3 5.3 %constant_dynamic-slice_fusion.3 = (bf16[2112,1,128]{2,1,0:T(2,128)(2,1)}, bf16[2112,1,128]{2,1,0:T(2,128)(2,1)S(1)}, bf16[2112,1,128]{2,1,0:T(2,128)(2,1)S(1)}, bf16[2112,1,128]{2,1,0:T(2,128)(2,1)S(1)}) fusion(bf16[2112,4,128]{2,1,0:T(4,128)(2,1)S(1)} %reshape.543, s32[]{:T(128)S(6)} %select_n.317, s32[]{:T(128)S(6)} %select_n.359, s32[]{:T(128)S(6)} %select_n.357, ...), kind=kLoop, calls=%fused_computation.232 | loop fusion | bytes 4325392 | tf_op jit(solution)/shard_map/dynamic-slice.7
  404.5 14.1 %collective-permute-start.46 = (bf16[2112,128]{1,0:T(8,128)(2,1)}, bf16[2112,128]{1,0:T(8,128)(2,1)}, u32[]{:S(2)}, u32[]{:S(2)}) collective-permute-start(bf16[2112,128]{1,0:T(8,128)(2,1)} %bitcast.374), channel_id=1, source_target_pairs={{0,8},{8,16},{16,24},{24,0},{1,9},{9,17},{17,25},{25,1},{2,10},{10... | collective-permute-start | bytes 1622024 | tf_op jit(solution)/shard_map/ppermute | solution.py:36
  435.0 16.4 %collective-permute-done.47 = bf16[2112,128]{1,0:T(8,128)(2,1)} collective-permute-done((bf16[2112,128]{1,0:T(8,128)(2,1)}, bf16[2112,128]{1,0:T(8,128)(2,1)}, u32[]{:S(2)}, u32[]{:S(2)}) %collective-permute-start.47) | collective-permute-done | bytes 540704 | tf_op jit(solution)/shard_map/ppermute | solution.py:36
  457.0 11.9 %collective-permute-start.36 = (bf16[216,128]{1,0:T(8,128)(2,1)S(1)}, bf16[216,128]{1,0:T(8,128)(2,1)S(1)}, u32[]{:S(2)}, u32[]{:S(2)}) collective-permute-start(bf16[216,128]{1,0:T(8,128)(2,1)S(1)} %get-tuple-element.128), channel_id=1, source_target_pairs={{0,8},{8,16},{16,24},{24,0},{1,9},{9,17},{17,25},{25,1},{2,10},{10... | collective-permute-start | bytes 165896 | tf_op jit(solution)/shard_map/ppermute | solution.py:36
  468.9 3.4 collective-permute-start.37
  (438 shorter events, 236.3 us)
Async XLA Ops:
  3.2 18.5 %collective-permute-start = (bf16[216,128]{1,0:T(8,128)(2,1)S(1)}, bf16[216,128]{1,0:T(8,128)(2,1)S(1)}, u32[]{:S(2)}, u32[]{:S(2)}) collective-permute-start(bf16[216,128]{1,0:T(8,128)(2,1)S(1)} %pad_maximum_fusion.27), channel_id=1, source_target_pairs={{0,8},{8,16},{16,24},{24,0},{1,9},{9,17},{17,25},{25,1},{2,10},{10... | collective-permute-start | bytes 165896 | tf_op jit(solution)/shard_map/ppermute | solution.py:36
  23.6 18.7 %collective-permute-start.9 = (bf16[2368,128]{1,0:T(8,128)(2,1)}, bf16[2368,128]{1,0:T(8,128)(2,1)S(1)}, u32[]{:S(2)}, u32[]{:S(2)}) collective-permute-start(bf16[2368,128]{1,0:T(8,128)(2,1)} %pad_maximum_fusion.16), channel_id=1, source_target_pairs={{0,8},{8,16},{16,24},{24,0},{1,9},{9,17},{17,25},{25,1},{2,10},{10... | collective-permute-start | bytes 1818632 | tf_op jit(solution)/shard_map/ppermute | solution.py:36
  24.3 42.1 %collective-permute-start.10 = (bf16[2368,128]{1,0:T(8,128)(2,1)}, bf16[2368,128]{1,0:T(8,128)(2,1)S(1)}, u32[]{:S(2)}, u32[]{:S(2)}) collective-permute-start(bf16[2368,128]{1,0:T(8,128)(2,1)} %pad_maximum_fusion.16), channel_id=1, source_target_pairs={{0,16},{8,24},{16,0},{24,8},{1,17},{9,25},{17,1},{25,9},{2,18},{10... | collective-permute-start | bytes 1818632 | tf_op jit(solution)/shard_map/ppermute | solution.py:36
  24.6 41.8 %collective-permute-start.11 = (bf16[2368,128]{1,0:T(8,128)(2,1)}, bf16[2368,128]{1,0:T(8,128)(2,1)S(1)}, u32[]{:S(2)}, u32[]{:S(2)}) collective-permute-start(bf16[2368,128]{1,0:T(8,128)(2,1)} %pad_maximum_fusion.16), channel_id=1, source_target_pairs={{0,24},{8,0},{16,8},{24,16},{1,25},{9,1},{17,9},{25,17},{2,26},{10... | collective-permute-start | bytes 1818632 | tf_op jit(solution)/shard_map/ppermute | solution.py:36
  34.6 33.5 %collective-permute-start.4 = (bf16[2,4,216,128]{3,2,0,1:T(8,128)(2,1)S(1)}, bf16[2,4,216,128]{3,2,0,1:T(8,128)(2,1)S(1)}, u32[]{:S(2)}, u32[]{:S(2)}) collective-permute-start(bf16[2,4,216,128]{3,2,0,1:T(8,128)(2,1)S(1)} %pad_maximum_fusion.20), channel_id=1, source_target_pairs={{0,2},{1,3},{2,0},{3,1},{4,6},{5,7},{6,4},{7,5},{8,10},{9,11},{10,... | collective-permute-start | bytes 1327112 | tf_op jit(solution)/shard_map/ppermute | solution.py:40
  66.5 53.5 %collective-permute-start.12 = (bf16[4,2368,128]{2,1,0:T(8,128)(2,1)S(1)}, bf16[4,2368,128]{2,1,0:T(8,128)(2,1)}, u32[]{:S(2)}, u32[]{:S(2)}) collective-permute-start(bf16[4,2368,128]{2,1,0:T(8,128)(2,1)S(1)} %bitcast_dynamic-update-slice_fusion), channel_id=1, source_target_pairs={{0,4},{4,0},{1,5},{5,1},{2,6},{6,2},{3,7},{7,3},{8,12},{12,8},{9,1... | collective-permute-start | bytes 7274504 | tf_op jit(solution)/shard_map/ppermute | solution.py:40
  140.8 56.5 %collective-permute-start.14 = (bf16[2,256,1024]{1,2,0:T(8,128)(2,1)}, bf16[2,256,1024]{1,2,0:T(8,128)(2,1)}, u32[]{:S(2)}, u32[]{:S(2)}) collective-permute-start(bf16[2,256,1024]{1,2,0:T(8,128)(2,1)} %pad_maximum_fusion.6), channel_id=1, source_target_pairs={{0,1},{1,0},{2,3},{3,2},{4,5},{5,4},{6,7},{7,6},{8,9},{9,8},{10,11... | collective-permute-start | bytes 3145736 | tf_op jit(solution)/shard_map/ppermute | solution.py:40
  142.9 16.1 %collective-permute-start.6 = (bf16[320,256]{1,0:T(8,128)(2,1)}, bf16[320,256]{1,0:T(8,128)(2,1)}, u32[]{:S(2)}, u32[]{:S(2)}) collective-permute-start(bf16[320,256]{1,0:T(8,128)(2,1)} %pad_maximum_fusion.23), channel_id=1, source_target_pairs={{0,3},{1,4},{2,5},{3,6},{4,7},{8,11},{9,12},{10,13},{11,14},{12,15... | collective-permute-start | bytes 491528 | tf_op jit(solution)/shard_map/ppermute | solution.py:384
  227.1 49.0 %collective-permute-start.24 = (bf16[256,1024]{1,0:T(8,128)(2,1)}, bf16[256,1024]{1,0:T(8,128)(2,1)}, u32[]{:S(2)}, u32[]{:S(2)}) collective-permute-start(bf16[256,1024]{1,0:T(8,128)(2,1)} %fusion.39), channel_id=1, source_target_pairs={{0,1},{1,0},{2,3},{3,2},{4,5},{5,4},{6,7},{7,6},{8,9},{9,8},{10,11... | collective-permute-start | bytes 1572872 | tf_op jit(solution)/shard_map/ppermute | solution.py:40
  229.4 32.8 %collective-permute-start.16 = (bf16[256,1024]{1,0:T(8,128)(2,1)}, bf16[256,1024]{1,0:T(8,128)(2,1)}, u32[]{:S(2)}, u32[]{:S(2)}) collective-permute-start(bf16[256,1024]{1,0:T(8,128)(2,1)} %fusion.37), channel_id=1, source_target_pairs={{0,1},{1,0},{2,3},{3,2},{4,5},{5,4},{6,7},{7,6},{8,9},{9,8},{10,11... | collective-permute-start | bytes 1572872 | tf_op jit(solution)/shard_map/ppermute | solution.py:40
  258.8 25.0 %collective-permute-start.26 = (bf16[256,1024]{1,0:T(8,128)(2,1)S(1)}, bf16[256,1024]{1,0:T(8,128)(2,1)S(1)}, u32[]{:S(2)}, u32[]{:S(2)}) collective-permute-start(bf16[256,1024]{1,0:T(8,128)(2,1)S(1)} %fusion.13), channel_id=1, source_target_pairs={{0,2},{1,3},{2,0},{3,1},{4,6},{5,7},{6,4},{7,5},{8,10},{9,11},{10,... | collective-permute-start | bytes 1572872 | tf_op jit(solution)/shard_map/ppermute | solution.py:40
  275.2 66.0 %collective-permute-start.21 = (bf16[256,1024]{1,0:T(8,128)(2,1)}, bf16[256,1024]{1,0:T(8,128)(2,1)}, u32[]{:S(2)}, u32[]{:S(2)}) collective-permute-start(bf16[256,1024]{1,0:T(8,128)(2,1)} %get-tuple-element.73), channel_id=1, source_target_pairs={{0,1},{1,0},{2,3},{3,2},{4,5},{5,4},{6,7},{7,6},{8,9},{9,8},{10,11... | collective-permute-start | bytes 1572872 | tf_op jit(solution)/shard_map/ppermute | solution.py:40
  275.2 70.9 %collective-permute-start.22 = (bf16[256,1024]{1,0:T(8,128)(2,1)}, bf16[256,1024]{1,0:T(8,128)(2,1)}, u32[]{:S(2)}, u32[]{:S(2)}) collective-permute-start(bf16[256,1024]{1,0:T(8,128)(2,1)} %get-tuple-element.73), channel_id=1, source_target_pairs={{0,2},{1,3},{2,0},{3,1},{4,6},{5,7},{6,4},{7,5},{8,10},{9,11},{10,... | collective-permute-start | bytes 1572872 | tf_op jit(solution)/shard_map/ppermute | solution.py:40
  326.1 29.4 %collective-permute-start.39 = (bf16[2,256,1024]{2,1,0:T(8,128)(2,1)}, bf16[2,256,1024]{2,1,0:T(8,128)(2,1)}, u32[]{:S(2)}, u32[]{:S(2)}) collective-permute-start(bf16[2,256,1024]{2,1,0:T(8,128)(2,1)} %fusion.7), channel_id=1, source_target_pairs={{0,1},{1,0},{2,3},{3,2},{4,5},{5,4},{6,7},{7,6},{8,9},{9,8},{10,11... | collective-permute-start | bytes 3145736 | tf_op jit(solution)/shard_map/ppermute | solution.py:40
  342.6 49.7 %collective-permute-start.45 = (bf16[2112,512]{1,0:T(8,128)(2,1)S(1)}, bf16[2112,512]{1,0:T(8,128)(2,1)S(1)}, u32[]{:S(2)}, u32[]{:S(2)}) collective-permute-start(bf16[2112,512]{1,0:T(8,128)(2,1)S(1)} %copy-done.35), channel_id=1, source_target_pairs={{0,4},{4,0},{1,5},{5,1},{2,6},{6,2},{3,7},{7,3},{8,12},{12,8},{9,1... | collective-permute-start | bytes 6488072 | tf_op jit(solution)/shard_map/ppermute | solution.py:40
  351.6 68.7 %collective-permute-start.32 = (bf16[256,1024]{1,0:T(8,128)(2,1)}, bf16[256,1024]{1,0:T(8,128)(2,1)}, u32[]{:S(2)}, u32[]{:S(2)}) collective-permute-start(bf16[256,1024]{1,0:T(8,128)(2,1)} %collective-permute-done.31), channel_id=1, source_target_pairs={{0,1},{1,0},{2,3},{3,2},{4,5},{5,4},{6,7},{7,6},{8,9},{9,8},{10,11... | collective-permute-start | bytes 1572872 | tf_op jit(solution)/shard_map/ppermute | solution.py:40
  358.1 72.5 %collective-permute-start.40 = (bf16[256,1024]{1,0:T(8,128)(2,1)}, bf16[256,1024]{1,0:T(8,128)(2,1)}, u32[]{:S(2)}, u32[]{:S(2)}) collective-permute-start(bf16[256,1024]{1,0:T(8,128)(2,1)} %fusion.41), channel_id=1, source_target_pairs={{0,2},{1,3},{2,0},{3,1},{4,6},{5,7},{6,4},{7,5},{8,10},{9,11},{10,... | collective-permute-start | bytes 1572872 | tf_op jit(solution)/shard_map/ppermute | solution.py:40
  360.1 66.7 %collective-permute-start.34 = (bf16[2,4,216,128]{3,2,1,0:T(8,128)(2,1)S(1)}, bf16[2,4,216,128]{3,2,1,0:T(8,128)(2,1)}, u32[]{:S(2)}, u32[]{:S(2)}) collective-permute-start(bf16[2,4,216,128]{3,2,1,0:T(8,128)(2,1)S(1)} %fusion.51), channel_id=1, source_target_pairs={{0,2},{1,3},{2,0},{3,1},{4,6},{5,7},{6,4},{7,5},{8,10},{9,11},{10,... | collective-permute-start | bytes 1327112 | tf_op jit(solution)/shard_map/ppermute | solution.py:40
  404.5 30.5 %collective-permute-start.46 = (bf16[2112,128]{1,0:T(8,128)(2,1)}, bf16[2112,128]{1,0:T(8,128)(2,1)}, u32[]{:S(2)}, u32[]{:S(2)}) collective-permute-start(bf16[2112,128]{1,0:T(8,128)(2,1)} %bitcast.374), channel_id=1, source_target_pairs={{0,8},{8,16},{16,24},{24,0},{1,9},{9,17},{17,25},{25,1},{2,10},{10... | collective-permute-start | bytes 1622024 | tf_op jit(solution)/shard_map/ppermute | solution.py:36
  419.4 32.0 %collective-permute-start.47 = (bf16[2112,128]{1,0:T(8,128)(2,1)}, bf16[2112,128]{1,0:T(8,128)(2,1)}, u32[]{:S(2)}, u32[]{:S(2)}) collective-permute-start(bf16[2112,128]{1,0:T(8,128)(2,1)} %bitcast.373), channel_id=1, source_target_pairs={{0,16},{8,24},{16,0},{24,8},{1,17},{9,25},{17,1},{25,9},{2,18},{10... | collective-permute-start | bytes 1622024 | tf_op jit(solution)/shard_map/ppermute | solution.py:36
  420.3 33.2 %collective-permute-start.48 = (bf16[2112,128]{1,0:T(8,128)(2,1)}, bf16[2112,128]{1,0:T(8,128)(2,1)}, u32[]{:S(2)}, u32[]{:S(2)}) collective-permute-start(bf16[2112,128]{1,0:T(8,128)(2,1)} %bitcast.372), channel_id=1, source_target_pairs={{0,24},{8,0},{16,8},{24,16},{1,25},{9,1},{17,9},{25,17},{2,26},{10... | collective-permute-start | bytes 1622024 | tf_op jit(solution)/shard_map/ppermute | solution.py:36
  428.9 27.1 %collective-permute-start.35 = (bf16[4,216,128]{2,1,0:T(8,128)(2,1)}, bf16[4,216,128]{2,1,0:T(8,128)(2,1)}, u32[]{:S(2)}, u32[]{:S(2)}) collective-permute-start(bf16[4,216,128]{2,1,0:T(8,128)(2,1)} %fusion.59), channel_id=1, source_target_pairs={{0,4},{4,0},{1,5},{5,1},{2,6},{6,2},{3,7},{7,3},{8,12},{12,8},{9,1... | collective-permute-start | bytes 663560 | tf_op jit(solution)/shard_map/ppermute | solution.py:40
  433.7 43.4 %collective-permute-start.41 = (bf16[256,512]{0,1:T(8,128)(2,1)S(1)}, bf16[256,512]{0,1:T(8,128)(2,1)}, u32[]{:S(2)}, u32[]{:S(2)}) collective-permute-start(bf16[256,512]{0,1:T(8,128)(2,1)S(1)} %bitcast.432), channel_id=1, source_target_pairs={{0,4},{4,0},{1,5},{5,1},{2,6},{6,2},{3,7},{7,3},{8,12},{12,8},{9,1... | collective-permute-start | bytes 786440 | tf_op jit(solution)/shard_map/ppermute | solution.py:40
  457.0 17.3 %collective-permute-start.36 = (bf16[216,128]{1,0:T(8,128)(2,1)S(1)}, bf16[216,128]{1,0:T(8,128)(2,1)S(1)}, u32[]{:S(2)}, u32[]{:S(2)}) collective-permute-start(bf16[216,128]{1,0:T(8,128)(2,1)S(1)} %get-tuple-element.128), channel_id=1, source_target_pairs={{0,8},{8,16},{16,24},{24,0},{1,9},{9,17},{17,25},{25,1},{2,10},{10... | collective-permute-start | bytes 165896 | tf_op jit(solution)/shard_map/ppermute | solution.py:36
  (105 other events, 761.5 us)
